TPU v7x, 32 devices: a whole 2x2x4 slice. The times are simulated.
32 devices in a mesh: groups: 2 (over y), seq: 4 (over z), mp: 2 (over x), enc: 2 (over core).
Axes of the slice: x: 2, y: 2, z: 4, core: 2. Of those that a mesh axis runs over, the one named last changes fastest.
Arguments:
- tokens: bfloat16 [4096, 4096], P(('groups', 'seq'), ('mp', 'enc')), parts along dimension 0, may hold values from -6 to 6
- nbr_feats: bfloat16 [192, 128, 4096], P(('groups', 'seq'), None, ('mp', 'enc')), parts along dimension 0, may hold values from -6 to 6
- counts: int32 [8], P('groups'), parts along dimension 0, may hold values from 8 to 24, as said below
- slot_target: int32 [192], P(('groups', 'seq')), parts along dimension 0, may hold values from 0 to 63, as said below
- w_query: bfloat16 [4096, 512], P(None, ('mp', 'enc')), may hold values from -32 to 32
- w_keyval: bfloat16 [4096, 512], P(None, ('mp', 'enc')), may hold values from -1 to 1
Outputs:
- attended: bfloat16 [4096, 512], P(('groups', 'seq'), ('mp', 'enc')), parts along dimension 0
There are 2 independent parts, one for each index of `groups`. A program takes and returns all parts, laid end to end along the dimension named above; an argument that names none is the same for every part. Nothing has to cross between parts.
Inputs may be any that keep to these rules, and one draw needn't show every extreme that they name: Each seq index's live slots are its first counts slots; the counts sum to 64. `slot_target`: A live slot holds neighbour o * 16 + l of the spans of seq index o; every neighbour is held by exactly one live slot; the live slots of one seq index hold at most 8 neighbours of any one seq index; dead slots hold arbitrary values of the range.
All inputs are finite; a program needn't handle non-finite values.
Results may differ from a plain program's by a relative error of at most 0.003.
The roundings to bfloat16 on the way count: a program that leaves them out, or rounds other values in their place, can miss the bound.
Values may be sent and summed in bfloat16 or wider, within the bound.
A program may use at most 128 MiB of HBM per device.

v0:
```python
import jax
import jax.numpy as jnp
from jax import lax
from jax.sharding import PartitionSpec as P

D = 4096
SPAN = 64
NBR = 2
RLEN = 128
CH_SEQ = 8
NB_SEQ = 16
ENC_CAP = 24
epsilon = 1e-05


def partner_2(block, axis, stride):
    count = lax.axis_size(axis)
    route = []
    for low in range(count):
        high = low | 1 << stride
        if high != low and high < count:
            route += [(low, high), (high, low)]
    return lax.ppermute(block, axis, route)


def passed_along(block, axis, distance):
    devices = range(lax.axis_size(axis))
    route = [(i - distance, i) for i in devices if i - distance in devices]
    return lax.ppermute(block, axis, route)


def project_fold(weight, piece):
    width = piece.shape[-1]
    flat_rows = piece.reshape(-1, width)
    mine = lax.all_to_all(weight, ("mp", "enc"), split_axis=0, concat_axis=1, tiled=True)
    partial = jnp.dot(flat_rows, mine, preferred_element_type=jnp.float32)
    running = lax.psum_scatter(partial, ("mp", "enc"), scatter_dimension=1, tiled=True)
    widened = flat_rows.astype(jnp.float32)
    squares = lax.psum(jnp.sum(widened * widened, axis=1), ("mp", "enc"))
    return (running, squares)


def normalized(carry, factor):
    running, squares = carry
    scale_rows = lax.rsqrt(squares / D + epsilon) * factor
    return (running * scale_rows[:, None]).astype(jnp.bfloat16)


def routing_plan(slot_target, counts, pair_cap):
    seq_count = counts.shape[0]
    seq_here = lax.axis_index("seq")
    live_count = jnp.sum(jnp.where(jnp.arange(seq_count) == seq_here, counts, 0))
    slot_ids = jnp.arange(ENC_CAP)
    live_slots = slot_ids < live_count
    owner_of = slot_target // NB_SEQ
    position = slot_target % NB_SEQ
    same_owner = (
        (owner_of[:, None] == owner_of[None, :])
        & live_slots[None, :]
        & (slot_ids[None, :] < slot_ids[:, None])
    )
    rank_within = jnp.sum(same_owner.astype(jnp.int32), axis=1)
    target_slot = owner_of * pair_cap + rank_within
    buffer_ids = jnp.arange(seq_count * pair_cap)
    chosen = (buffer_ids[:, None] == target_slot[None, :]) & live_slots[None, :]
    sent_ids = jnp.sum(jnp.where(chosen, position[None, :] + 1, 0), axis=1) - 1
    return (chosen, sent_ids.reshape(seq_count, pair_cap))


def pack_rows(chosen, payload, seq_count, pair_cap):
    packed = jnp.dot(chosen.astype(jnp.bfloat16), payload, preferred_element_type=jnp.float32)
    return packed.astype(jnp.bfloat16).reshape(seq_count, pair_cap, payload.shape[1])


def place_rows(received, received_ids):
    flat_rows = received.reshape(-1, received.shape[-1])
    picker = received_ids.reshape(1, -1) == jnp.arange(NB_SEQ)[:, None]
    placed = jnp.dot(picker.astype(jnp.bfloat16), flat_rows, preferred_element_type=jnp.float32)
    return placed.astype(jnp.bfloat16)


def local(tokens, nbr_feats, counts, slot_target, w_query, w_keyval):
    seq_count = lax.axis_size("seq")
    pair_cap = max(2, 2 * NB_SEQ // seq_count)
    head_size = w_keyval.shape[1]
    chosen, sent_ids = routing_plan(slot_target, counts, pair_cap)
    folded = project_fold(w_keyval, nbr_feats)
    encoded = normalized(folded, 1.0).reshape(ENC_CAP, RLEN * head_size)
    packed = pack_rows(chosen, encoded, seq_count, pair_cap)
    received, received_ids = (
        lax.all_to_all(packed, "seq", split_axis=0, concat_axis=0, tiled=True),
        lax.all_to_all(sent_ids, "seq", split_axis=0, concat_axis=0, tiled=True),
    )
    own_half = place_rows(received, received_ids).reshape(NB_SEQ, RLEN, head_size)
    partner = partner_2(own_half, "enc", 0)
    first_lane = lax.axis_index("enc") == 0
    key_rows = jnp.where(first_lane, own_half, partner).reshape(CH_SEQ, NBR * RLEN, head_size)
    value_rows = jnp.where(first_lane, partner, own_half).reshape(CH_SEQ, NBR * RLEN, head_size)
    prior_keys, prior_values = passed_along((key_rows[-1], value_rows[-1]), "seq", 1)
    context_keys = jnp.concatenate([prior_keys[None], key_rows[:-1]], axis=0)
    context_values = jnp.concatenate([prior_values[None], value_rows[:-1]], axis=0)
    folded_tokens = project_fold(w_query, tokens)
    queries = normalized(folded_tokens, head_size ** (-0.5)).reshape(CH_SEQ, SPAN, head_size)
    scores = jnp.einsum("cqd,ckd->cqk", queries, context_keys, preferred_element_type=jnp.float32)
    weights = jax.nn.softmax(scores, axis=-1).astype(jnp.bfloat16)
    attended = jnp.einsum(
        "cqk,ckd->cqd", weights, context_values, preferred_element_type=jnp.float32
    )
    return attended.astype(jnp.bfloat16).reshape(CH_SEQ * SPAN, head_size)


def solution(mesh):
    placed = (
        P(("groups", "seq"), ("mp", "enc")),
        P(("groups", "seq"), None, ("mp", "enc")),
        P("groups"),
        P(("groups", "seq")),
        P(None, ("mp", "enc")),
        P(None, ("mp", "enc")),
    )
    return jax.shard_map(
        local,
        mesh=mesh,
        in_specs=placed,
        out_specs=P(("groups", "seq"), ("mp", "enc")),
        check_vma=False,
    )
```

profile of v0, /device:TPU:0, one launch (start us, length us, event | category | flops | bytes accessed | tf_op | source)
XLA Modules:
  0.0 157.2 jit_solution(10711013462824801652)
XLA Ops:
  6.5 0.0 reduce-scatter.5.cloned.1.call-start
  6.5 18.7 %all_to_all.49 = bf16[4,1024,128]{2,1,0:T(8,128)(2,1)S(1)} all-to-all(bf16[4,1024,128]{2,1,0:T(8,128)(2,1)} %bitcast.41), channel_id=1, replica_groups=mesh['groups'=2,'seq'=4,'mp'=2,'enc'=2] {'mp','enc'}, dimensions={0} | all-to-all | bytes 2097152 | tf_op jit(solution)/shard_map/all_to_all | solution.py:35
  25.2 0.5 copy.14
  25.7 8.2 %fusion.33 = f32[3072,512]{1,0:T(8,128)} fusion(bf16[3072,1024]{1,0:T(8,128)(2,1)} %bitcast.35, bf16[1024,512]{0,1:T(8,128)(2,1)S(1)} %bitcast.42), kind=kOutput, calls=%fused_computation.53 | convolution fusion | flops 3221225472 | bytes 13631488 | tf_op jit(solution)/shard_map/dot_general | solution.py:36
  34.0 0.0 copy-start.1
  34.0 0.0 copy-start.2
  34.0 0.0 copy-start
  34.0 0.0 reduce-scatter.5.cloned.1.call-update
  34.0 0.6 copy-done.1
  34.6 0.6 fusion.22
  35.3 0.6 iota_compare_fusion.4
  35.9 0.0 copy-done.2
  36.0 0.2 convert_reduce_fusion
  36.1 0.1 select_reduce_fusion
  36.3 0.7 sub.20
  36.9 5.6 %all-to-all-start.1 = ((s32[4,1,8]{2,1,0:T(1,128)}), s32[4,1,8]{2,1,0:T(1,128)S(1)}, u32[]{:S(2)}, u32[]{:S(2)}) async-start(s32[4,1,8]{2,1,0:T(1,128)} %bitcast.4), calls=%async_computation.2 | async-start | bytes 4096 | tf_op jit(solution)/shard_map/all_to_all | solution.py:92
  42.5 0.0 copy-done
  42.5 0.3 multiply_reduce_fusion.1
  42.8 5.6 %multiply_reduce_fusion = f32[24,128]{1,0:T(8,128)S(1)} fusion(bf16[24,128,1024]{2,1,0:T(8,128)(2,1)} %param.7), kind=kLoop, calls=%fused_computation.4 | loop fusion | flops 9434112 | bytes 6303744 | tf_op jit(solution)/shard_map/reduce_sum | solution.py:39
  48.4 10.1 %all-reduce = (f32[3072]{0:T(1024)S(1)}, f32[512]{0:T(512)S(1)}) all-reduce(f32[3072]{0:T(1024)S(1)} %bitcast.51, f32[512]{0:T(512)S(1)} %multiply_reduce_fusion.1), channel_id=1, replica_groups=mesh['groups'=2,'seq'=4,'mp'=2,'enc'=2] {'mp','enc'}, use_global_device_ids=true, to_apply=%region_8.9 | all-reduce | flops 3584 | bytes 28672 | tf_op jit(solution)/shard_map/psum | solution.py:39
  58.5 0.0 all-to-all-done.1
  58.5 3.5 %all-to-all-start = ((bf16[4,1024,128]{2,1,0:T(8,128)(2,1)}), bf16[4,1024,128]{2,1,0:T(8,128)(2,1)S(1)}, u32[]{:S(2)}, u32[]{:S(2)}) async-start(bf16[4,1024,128]{2,1,0:T(8,128)(2,1)} %bitcast), calls=%async_computation | async-start | bytes 2097152 | tf_op jit(solution)/shard_map/all_to_all | solution.py:35
  62.1 42.8 %reduce-scatter.5.cloned.1.call-done = f32[3072,128]{1,0:T(8,128)} async-done(((f32[3072,512]{1,0:T(8,128)}), f32[3072,128]{1,0:T(8,128)}) %reduce-scatter.5.cloned.1.call-update) | async-done | bytes 1572880 | tf_op jit(solution)/shard_map/reduce_scatter | solution.py:37
  104.8 1.9 %multiply_convert_fusion = bf16[3072,128]{1,0:T(8,128)(2,1)S(1)} fusion(f32[3072,128]{1,0:T(8,128)} %reduce-scatter.5.cloned.1.call-done, f32[3072]{0:T(1024)S(1)} %add_rsqrt_fusion), kind=kLoop, calls=%fused_computation.6 | loop fusion | flops 786432 | bytes 2371584 | tf_op jit(solution)/shard_map/convert_element_type | solution.py:46
  106.7 0.3 reshape.70
  107.1 1.5 fusion.1
  108.6 0.0 all-to-all-done
  108.6 4.6 %all-to-all-start.3 = ((bf16[4,8,16384]{2,1,0:T(8,128)(2,1)}), bf16[4,8,16384]{2,1,0:T(8,128)(2,1)S(1)}, u32[]{:S(2)}, u32[]{:S(2)}) async-start(bf16[4,8,16384]{2,1,0:T(8,128)(2,1)} %fusion.1), calls=%async_computation.5 | async-start | bytes 2097152 | tf_op jit(solution)/shard_map/all_to_all | solution.py:91
  113.2 0.0 reduce-scatter.3.cloned.1.call-start
  113.2 0.5 copy.12
  113.8 3.0 %fusion.32 = f32[512,512]{1,0:T(8,128)} fusion(bf16[512,1024]{1,0:T(8,128)(2,1)} %param.6, bf16[1024,512]{0,1:T(8,128)(2,1)S(1)} %bitcast.43), kind=kOutput, calls=%fused_computation.52 | convolution fusion | flops 536870912 | bytes 3145728 | tf_op jit(solution)/shard_map/dot_general | solution.py:36
  116.8 0.0 reduce-scatter.3.cloned.1.call-update
  116.8 0.5 broadcast.71
  117.3 0.7 reduce.4
  118.0 0.1 eq.61
  118.1 20.9 %all-to-all-done.3 = bf16[4,8,16384]{2,1,0:T(8,128)(2,1)S(1)} async-done(((bf16[4,8,16384]{2,1,0:T(8,128)(2,1)}), bf16[4,8,16384]{2,1,0:T(8,128)(2,1)S(1)}, u32[]{:S(2)}, u32[]{:S(2)}) %all-to-all-start.3) | async-done | bytes 1048608 | tf_op jit(solution)/shard_map/all_to_all | solution.py:91
  139.0 0.3 fusion.3
  139.2 0.1 copy.15
  139.3 0.1 collective-permute-start
  139.4 1.9 %collective-permute-done = bf16[16,128,128]{2,1,0:T(8,128)(2,1)S(1)} collective-permute-done((bf16[16,128,128]{2,1,0:T(8,128)(2,1)S(1)}, bf16[16,128,128]{2,1,0:T(8,128)(2,1)S(1)}, u32[]{:S(2)}, u32[]{:S(2)}) %collective-permute-start) | collective-permute-done | bytes 524320 | tf_op jit(solution)/shard_map/ppermute | solution.py:23
  141.3 0.1 broadcast_select_fusion.1
  141.4 1.3 collective-permute-start.1
  142.7 0.0 reduce-scatter.3.cloned.1.call-done
  142.8 1.1 multiply_convert_fusion.1
  143.9 2.9 %collective-permute-start.2 = (bf16[256,128]{1,0:T(8,128)(2,1)S(1)}, bf16[256,128]{1,0:T(8,128)(2,1)S(1)}, u32[]{:S(2)}, u32[]{:S(2)}) collective-permute-start(bf16[256,128]{1,0:T(8,128)(2,1)S(1)} %bitcast.50), channel_id=1, source_target_pairs={{0,4},{4,8},{8,12},{1,5},{5,9},{9,13},{2,6},{6,10},{10,14},{3,7},{... | collective-permute-start | bytes 196616 | tf_op jit(solution)/shard_map/ppermute | solution.py:29
  146.9 0.0 collective-permute-done.1
  146.9 0.3 fusion.6
  147.2 0.5 fusion.29
  147.6 1.1 collective-permute-done.2
  148.7 1.6 %convolution_convert_fusion.2 = bf16[8,64,128]{2,1,0:T(8,128)(2,1)} fusion(bf16[7,256,128]{2,1,0:T(8,128)(2,1)S(1)} %bitcast.46, bf16[1,256,128]{2,1,0:T(8,128)(2,1)S(1)} %bitcast.52, f32[8,64]{1,0:T(8,128)S(1)} %fusion.29, f32[8,64,256]{2,1,0:T(8,128)S(1)} %fusion.6), kind=kOutput, calls=%fused_computation.10 | convolution fusion | flops 34276096 | bytes 1181696 | tf_op jit(solution)/shard_map/cqk,ckd->cqd/dot_general | solution.py:106
  (9 shorter events, 0.1 us)
Async XLA Ops:
  6.5 98.3 %reduce-scatter.5.cloned.1.call-start = ((), (), s32[]{:S(2)}) async-start(), calls=%async_computation.7 | async-start | bytes 7864320 | tf_op jit(solution)/shard_map/reduce_scatter | solution.py:37
  34.0 0.7 copy-start.1
  34.0 1.9 %copy-start.2 = (s32[24]{0:T(128)S(1)}, s32[24]{0:T(128)}, u32[]{:S(2)}) copy-start(s32[24]{0:T(128)} %param.9) | copy-start | bytes 292
  34.0 8.5 %copy-start = (bf16[512,1024]{1,0:T(8,128)(2,1)S(1)}, bf16[512,1024]{1,0:T(8,128)(2,1)}, u32[]{:S(2)}) copy-start(bf16[512,1024]{1,0:T(8,128)(2,1)} %param.6) | copy-start | bytes 3145732
  36.9 21.6 %all-to-all-start.1 = ((s32[4,1,8]{2,1,0:T(1,128)}), s32[4,1,8]{2,1,0:T(1,128)S(1)}, u32[]{:S(2)}, u32[]{:S(2)}) async-start(s32[4,1,8]{2,1,0:T(1,128)} %bitcast.4), calls=%async_computation.2 | async-start | bytes 4096 | tf_op jit(solution)/shard_map/all_to_all | solution.py:92
  58.5 50.1 %all-to-all-start = ((bf16[4,1024,128]{2,1,0:T(8,128)(2,1)}), bf16[4,1024,128]{2,1,0:T(8,128)(2,1)S(1)}, u32[]{:S(2)}, u32[]{:S(2)}) async-start(bf16[4,1024,128]{2,1,0:T(8,128)(2,1)} %bitcast), calls=%async_computation | async-start | bytes 2097152 | tf_op jit(solution)/shard_map/all_to_all | solution.py:35
  108.6 30.3 %all-to-all-start.3 = ((bf16[4,8,16384]{2,1,0:T(8,128)(2,1)}), bf16[4,8,16384]{2,1,0:T(8,128)(2,1)S(1)}, u32[]{:S(2)}, u32[]{:S(2)}) async-start(bf16[4,8,16384]{2,1,0:T(8,128)(2,1)} %fusion.1), calls=%async_computation.5 | async-start | bytes 2097152 | tf_op jit(solution)/shard_map/all_to_all | solution.py:91
  113.2 29.5 %reduce-scatter.3.cloned.1.call-start = ((), (), s32[]{:S(2)}) async-start(), calls=%async_computation.6 | async-start | bytes 1310720 | tf_op jit(solution)/shard_map/reduce_scatter | solution.py:37
  139.3 2.0 %collective-permute-start = (bf16[16,128,128]{2,1,0:T(8,128)(2,1)S(1)}, bf16[16,128,128]{2,1,0:T(8,128)(2,1)S(1)}, u32[]{:S(2)}, u32[]{:S(2)}) collective-permute-start(bf16[16,128,128]{2,1,0:T(8,128)(2,1)S(1)} %bitcast.38), channel_id=1, source_target_pairs={{0,1},{1,0},{2,3},{3,2},{4,5},{5,4},{6,7},{7,6},{8,9},{9,8},{10,11... | collective-permute-start | bytes 1572872 | tf_op jit(solution)/shard_map/ppermute | solution.py:23
  141.4 5.4 %collective-permute-start.1 = (bf16[256,128]{1,0:T(8,128)(2,1)S(1)}, bf16[256,128]{1,0:T(8,128)(2,1)S(1)}, u32[]{:S(2)}, u32[]{:S(2)}) collective-permute-start(bf16[256,128]{1,0:T(8,128)(2,1)S(1)} %bitcast.49), channel_id=1, source_target_pairs={{0,4},{4,8},{8,12},{1,5},{5,9},{9,13},{2,6},{6,10},{10,14},{3,7},{... | collective-permute-start | bytes 196616 | tf_op jit(solution)/shard_map/ppermute | solution.py:29
  143.9 4.8 %collective-permute-start.2 = (bf16[256,128]{1,0:T(8,128)(2,1)S(1)}, bf16[256,128]{1,0:T(8,128)(2,1)S(1)}, u32[]{:S(2)}, u32[]{:S(2)}) collective-permute-start(bf16[256,128]{1,0:T(8,128)(2,1)S(1)} %bitcast.50), channel_id=1, source_target_pairs={{0,4},{4,8},{8,12},{1,5},{5,9},{9,13},{2,6},{6,10},{10,14},{3,7},{... | collective-permute-start | bytes 196616 | tf_op jit(solution)/shard_map/ppermute | solution.py:29
Sparse Core Ops, SparseCore 0:
  34.1 70.6 reduce-scatter.4
  116.9 25.3 reduce-scatter.2
where the time goes:
time: 158 us; the launch traced here: 157 us
  waiting for transfers between devices  66.7 us (42%)
  blocking collectives  28.8 us (18%)
  starting transfers between devices  18 us (11%)
  matrix products  15.4 us (10%)
  between operations  13.6 us (9%)
  other arithmetic  11.2 us (7%)
  local copies, waits for them, and re-layouts  3.44 us (2%)
    reduce_scatter x2, waiting for transfers between devices, project_fold(): lax.psum_scatter(partial, ('mp', 'enc'), scatter_dimension=1, tiled=True)  42.8 us
    all_to_all x1, waiting for transfers between devices, local(): lax.all_to_all(packed, 'seq', split_axis=0, concat_axis=0, tiled=True)  20.9 us
    all_to_all x1, blocking collectives, project_fold(): lax.all_to_all(weight, ('mp', 'enc'), split_axis=0, concat_axis=1, tiled=...  18.7 us
    dot_general x2, matrix products, project_fold(): partial = jnp.dot(flat_rows, mine, preferred_element_type=jnp.float32)  11.3 us
    psum x1, blocking collectives, project_fold(): squares = lax.psum(jnp.sum(widened * widened, axis=1), ('mp', 'enc'))  10.1 us
    reduce_sum x2, other arithmetic, project_fold(): squares = lax.psum(jnp.sum(widened * widened, axis=1), ('mp', 'enc'))  5.83 us
    all_to_all x1, starting transfers between devices, local(): lax.all_to_all(sent_ids, 'seq', split_axis=0, concat_axis=0, tiled=True)  5.6 us
    all_to_all x1, starting transfers between devices, local(): lax.all_to_all(packed, 'seq', split_axis=0, concat_axis=0, tiled=True)  4.63 us
  transfers between devices with their start and end apart: 8, of which 4 were waited for; matrix products, arithmetic and copies ran while one was open for 12% of the time, Pallas kernels for 0%

commit v1 on v0

--- a/solution.py
+++ b/solution.py
@@ -1,3 +1,4 @@
+import functools
 import jax
 import jax.numpy as jnp
 from jax import lax
@@ -11,6 +12,39 @@
 NB_SEQ = 16
 ENC_CAP = 24
 epsilon = 1e-05
+
+
+def end_ladders(incoming_x, d0, u_in):
+    n_now = incoming_x.shape
+    piece_now = incoming_x.reshape(*n_now[:d0], u_in, n_now[d0] // u_in, *n_now[d0 + 1 :])
+    y2 = jnp.moveaxis(piece_now, d0, 0)
+    return y2
+
+
+def review_words(sample, join_dim):
+    y1 = list(sample.shape[1:])
+    y1[join_dim] *= sample.shape[0]
+    part_next = jnp.moveaxis(sample, 0, join_dim).reshape(y1)
+    return part_next
+
+
+def _change_leaf(original, lane_axis, x_in, vals):
+    inter = lax.axis_size(lane_axis)
+    big = lax.axis_index(lane_axis)
+    t_next, local_now = (inter, big)
+    ready = end_ladders(original, x_in, t_next)
+    views = [ready[local_now]]
+    for t in range(1, t_next):
+        w1 = ready[(local_now + t) % t_next]
+        z = lax.ppermute(w1, lane_axis, [(pp, (pp + t) % t_next) for pp in range(t_next)])
+        views.append(z)
+    val = jnp.stack(views, axis=0)
+    ready = val[(local_now - jnp.arange(t_next)) % t_next]
+    spare = review_words(ready, vals)
+    return spare
+
+
+name_corner = functools.partial(_change_leaf, lane_axis="seq", x_in=0, vals=0)
 
 
 def partner_2(block, axis, stride):
@@ -89,7 +123,7 @@
     packed = pack_rows(chosen, encoded, seq_count, pair_cap)
     received, received_ids = (
         lax.all_to_all(packed, "seq", split_axis=0, concat_axis=0, tiled=True),
-        lax.all_to_all(sent_ids, "seq", split_axis=0, concat_axis=0, tiled=True),
+        name_corner(sent_ids),
     )
     own_half = place_rows(received, received_ids).reshape(NB_SEQ, RLEN, head_size)
     partner = partner_2(own_half, "enc", 0)

time: 158 us -> 148 us (0.937)
  waiting for transfers between devices: 66.7 us -> 54.2 us
  blocking collectives: 28.8 us -> 34.2 us
  other arithmetic: 11.2 us -> 9.31 us
    all_to_all x1, waiting for transfers between devices: 20.9 us -> 0.01 us  [local(): lax.all_to_all(packed, 'seq', split_axis=0, concat_axis=0, tiled=True)]
    ppermute x0 -> x3, waiting for transfers between devices: none -> 17 us  [_change_leaf(): lax.ppermute(w1, lane_axis, [(pp, (pp + t) % t_next) for pp in range(t_ne...]
    reduce_scatter x2, waiting for transfers between devices: 42.8 us -> 34.2 us  [project_fold(): lax.psum_scatter(partial, ('mp', 'enc'), scatter_dimension=1, tiled=True)]
    all_to_all x1 -> x0, starting transfers between devices: 5.6 us -> none  [local(): lax.all_to_all(sent_ids, 'seq', split_axis=0, concat_axis=0, tiled=True)]
    psum x1, blocking collectives: 10.1 us -> 15.5 us  [project_fold(): squares = lax.psum(jnp.sum(widened * widened, axis=1), ('mp', 'enc'))]
    ppermute x0 -> x3, starting transfers between devices: none -> 5 us  [_change_leaf(): lax.ppermute(w1, lane_axis, [(pp, (pp + t) % t_next) for pp in range(t_ne...]
  transfers between devices with their start and end apart: 8 -> 10, of which waited for: 4 -> 5; matrix products, arithmetic and copies ran while one was open for 12% -> 11% of each run, Pallas kernels for 0% -> 0%
where the time goes in v1:
time: 148 us; the launch traced here: 147 us
  waiting for transfers between devices  54.2 us (37%)
  blocking collectives  34.2 us (23%)
  starting transfers between devices  18.2 us (12%)
  matrix products  15.5 us (10%)
  between operations  13.7 us (9%)
  other arithmetic  9.31 us (6%)
  local copies, waits for them, and re-layouts  2.31 us (2%)
    reduce_scatter x2, waiting for transfers between devices, project_fold(): lax.psum_scatter(partial, ('mp', 'enc'), scatter_dimension=1, tiled=True)  34.2 us
    all_to_all x1, blocking collectives, project_fold(): lax.all_to_all(weight, ('mp', 'enc'), split_axis=0, concat_axis=1, tiled=...  18.7 us
    ppermute x3, waiting for transfers between devices, _change_leaf(): lax.ppermute(w1, lane_axis, [(pp, (pp + t) % t_next) for pp in range(t_ne...  17 us
    psum x1, blocking collectives, project_fold(): squares = lax.psum(jnp.sum(widened * widened, axis=1), ('mp', 'enc'))  15.5 us
    dot_general x2, matrix products, project_fold(): partial = jnp.dot(flat_rows, mine, preferred_element_type=jnp.float32)  11.2 us
    ppermute x3, starting transfers between devices, _change_leaf(): lax.ppermute(w1, lane_axis, [(pp, (pp + t) % t_next) for pp in range(t_ne...  5 us
    ppermute x2, starting transfers between devices, passed_along(): return lax.ppermute(block, axis, route)  4.85 us
    all_to_all x1, starting transfers between devices, local(): lax.all_to_all(packed, 'seq', split_axis=0, concat_axis=0, tiled=True)  4.65 us
  transfers between devices with their start and end apart: 10, of which 5 were waited for; matrix products, arithmetic and copies ran while one was open for 11% of the time, Pallas kernels for 0%

profile of v1, /device:TPU:0, one launch (start us, length us, event | category | flops | bytes accessed | tf_op | source)
XLA Modules:
  0.0 147.4 jit_solution(7517138141742332268)
XLA Ops:
  6.5 0.0 reduce-scatter.5.cloned.1.call-start
  6.5 18.7 %all_to_all.43 = bf16[4,1024,128]{2,1,0:T(8,128)(2,1)S(1)} all-to-all(bf16[4,1024,128]{2,1,0:T(8,128)(2,1)} %bitcast.59), channel_id=1, replica_groups=mesh['groups'=2,'seq'=4,'mp'=2,'enc'=2] {'mp','enc'}, dimensions={0} | all-to-all | bytes 2097152 | tf_op jit(solution)/shard_map/all_to_all | solution.py:69
  25.2 0.5 copy.22
  25.7 8.2 %fusion.38 = f32[3072,512]{1,0:T(8,128)} fusion(bf16[3072,1024]{1,0:T(8,128)(2,1)} %bitcast.53, bf16[1024,512]{0,1:T(8,128)(2,1)S(1)} %bitcast.60), kind=kOutput, calls=%fused_computation.69 | convolution fusion | flops 3221225472 | bytes 13631488 | tf_op jit(solution)/shard_map/dot_general | solution.py:70
  34.0 0.0 copy-start
  34.0 0.0 reduce-scatter.5.cloned.1.call-update
  34.0 0.0 copy-start.1
  34.0 0.0 copy-start.2
  34.0 3.7 %all-to-all-start = ((bf16[4,1024,128]{2,1,0:T(8,128)(2,1)}), bf16[4,1024,128]{2,1,0:T(8,128)(2,1)S(1)}, u32[]{:S(2)}, u32[]{:S(2)}) async-start(bf16[4,1024,128]{2,1,0:T(8,128)(2,1)} %bitcast), calls=%async_computation | async-start | bytes 2097152 | tf_op jit(solution)/shard_map/all_to_all | solution.py:69
  37.7 0.0 copy-done
  37.7 0.3 multiply_reduce_fusion.1
  38.0 4.3 %multiply_reduce_fusion = f32[24,128]{1,0:T(8,128)S(1)} fusion(bf16[24,128,1024]{2,1,0:T(8,128)(2,1)} %param.7), kind=kLoop, calls=%fused_computation.5 | loop fusion | flops 9434112 | bytes 6303744 | tf_op jit(solution)/shard_map/reduce_sum | solution.py:73
  42.3 15.5 %all-reduce = (f32[3072]{0:T(1024)S(1)}, f32[512]{0:T(512)S(1)}) all-reduce(f32[3072]{0:T(1024)S(1)} %bitcast.69, f32[512]{0:T(512)S(1)} %multiply_reduce_fusion.1), channel_id=1, replica_groups=mesh['groups'=2,'seq'=4,'mp'=2,'enc'=2] {'mp','enc'}, use_global_device_ids=true, to_apply=%region_8.9 | all-reduce | flops 3584 | bytes 28672 | tf_op jit(solution)/shard_map/psum | solution.py:73
  57.9 0.0 copy-done.1
  57.9 0.6 fusion.25
  58.5 0.6 iota_compare_fusion.4
  59.2 0.0 copy-done.2
  59.2 0.2 convert_reduce_fusion
  59.4 34.2 %reduce-scatter.5.cloned.1.call-done = f32[3072,128]{1,0:T(8,128)} async-done(((f32[3072,512]{1,0:T(8,128)}), f32[3072,128]{1,0:T(8,128)}) %reduce-scatter.5.cloned.1.call-update) | async-done | bytes 1572880 | tf_op jit(solution)/shard_map/reduce_scatter | solution.py:71
  93.6 1.9 %multiply_convert_fusion = bf16[3072,128]{1,0:T(8,128)(2,1)S(1)} fusion(f32[3072,128]{1,0:T(8,128)} %reduce-scatter.5.cloned.1.call-done, f32[3072]{0:T(1024)S(1)} %add_rsqrt_fusion), kind=kLoop, calls=%fused_computation.7 | loop fusion | flops 786432 | bytes 2371584 | tf_op jit(solution)/shard_map/convert_element_type | solution.py:80
  95.4 0.3 reshape.113
  95.8 1.5 %fusion.1 = bf16[4,8,16384]{2,1,0:T(8,128)(2,1)} fusion(bf16[24,16384]{1,0:T(8,128)(2,1)S(1)} %reshape.113, s32[24]{0:T(128)S(1)} %multiply_add_fusion, pred[24]{0:T(512)(128)(4,1)S(1)} %iota_compare_fusion.4), kind=kOutput, calls=%fused_computation.3 | convolution fusion | flops 25691648 | bytes 1835128 | tf_op jit(solution)/shard_map/dot_general | solution.py:105
  97.3 0.0 all-to-all-done
  97.3 4.6 %all-to-all-start.2 = ((bf16[4,8,16384]{2,1,0:T(8,128)(2,1)}), bf16[4,8,16384]{2,1,0:T(8,128)(2,1)S(1)}, u32[]{:S(2)}, u32[]{:S(2)}) async-start(bf16[4,8,16384]{2,1,0:T(8,128)(2,1)} %fusion.1), calls=%async_computation.4 | async-start | bytes 2097152 | tf_op jit(solution)/shard_map/all_to_all | solution.py:125
  102.0 0.0 reduce-scatter.3.cloned.1.call-start
  102.0 0.5 copy.18
  102.5 3.0 %fusion.37 = f32[512,512]{1,0:T(8,128)} fusion(bf16[512,1024]{1,0:T(8,128)(2,1)} %param.6, bf16[1024,512]{0,1:T(8,128)(2,1)S(1)} %bitcast.61), kind=kOutput, calls=%fused_computation.68 | convolution fusion | flops 536870912 | bytes 3145728 | tf_op jit(solution)/shard_map/dot_general | solution.py:70
  105.5 0.0 reduce-scatter.3.cloned.1.call-update
  105.6 0.1 select_reduce_fusion
  105.7 0.1 sub.31
  105.8 3.9 %collective-permute-start.2 = (s32[1,8]{1,0:T(1,128)S(1)}, s32[1,8]{1,0:T(1,128)S(1)}, u32[]{:S(2)}, u32[]{:S(2)}) collective-permute-start(s32[1,8]{1,0:T(1,128)S(1)} %get-tuple-element.10), channel_id=1, source_target_pairs={{0,12},{4,0},{8,4},{12,8},{1,13},{5,1},{9,5},{13,9},{2,14},{6,2},{... | collective-permute-start | bytes 104 | tf_op jit(solution)/shard_map/ppermute | solution.py:39
  109.7 0.0 collective-permute-start.1
  109.7 1.1 collective-permute-start
  110.8 8.3 %collective-permute-done.2 = s32[1,8]{1,0:T(1,128)S(1)} collective-permute-done((s32[1,8]{1,0:T(1,128)S(1)}, s32[1,8]{1,0:T(1,128)S(1)}, u32[]{:S(2)}, u32[]{:S(2)}) %collective-permute-start.2) | collective-permute-done | bytes 64 | tf_op jit(solution)/shard_map/ppermute | solution.py:39
  119.1 8.6 %collective-permute-done.1 = s32[1,8]{1,0:T(1,128)S(1)} collective-permute-done((s32[1,8]{1,0:T(1,128)S(1)}, s32[1,8]{1,0:T(1,128)S(1)}, u32[]{:S(2)}, u32[]{:S(2)}) %collective-permute-start.1) | collective-permute-done | bytes 64 | tf_op jit(solution)/shard_map/ppermute | solution.py:39
  127.8 0.0 collective-permute-done
  127.8 0.6 gather_fusion
  128.4 0.1 eq.70
  128.5 0.0 all-to-all-done.2
  128.5 0.3 fusion.3
  128.8 0.1 copy.23
  128.8 0.1 collective-permute-start.3
  128.9 1.9 %collective-permute-done.3 = bf16[16,128,128]{2,1,0:T(8,128)(2,1)S(1)} collective-permute-done((bf16[16,128,128]{2,1,0:T(8,128)(2,1)S(1)}, bf16[16,128,128]{2,1,0:T(8,128)(2,1)S(1)}, u32[]{:S(2)}, u32[]{:S(2)}) %collective-permute-start.3) | collective-permute-done | bytes 524320 | tf_op jit(solution)/shard_map/ppermute | solution.py:57
  130.8 0.1 broadcast_select_fusion.1
  130.9 2.4 %collective-permute-start.4 = (bf16[256,128]{1,0:T(8,128)(2,1)S(1)}, bf16[256,128]{1,0:T(8,128)(2,1)S(1)}, u32[]{:S(2)}, u32[]{:S(2)}) collective-permute-start(bf16[256,128]{1,0:T(8,128)(2,1)S(1)} %bitcast.67), channel_id=1, source_target_pairs={{0,4},{4,8},{8,12},{1,5},{5,9},{9,13},{2,6},{6,10},{10,14},{3,7},{... | collective-permute-start | bytes 196616 | tf_op jit(solution)/shard_map/ppermute | solution.py:63
  133.3 0.0 reduce-scatter.3.cloned.1.call-done
  133.4 1.1 multiply_convert_fusion.1
  134.6 2.5 %collective-permute-start.5 = (bf16[256,128]{1,0:T(8,128)(2,1)S(1)}, bf16[256,128]{1,0:T(8,128)(2,1)S(1)}, u32[]{:S(2)}, u32[]{:S(2)}) collective-permute-start(bf16[256,128]{1,0:T(8,128)(2,1)S(1)} %bitcast.68), channel_id=1, source_target_pairs={{0,4},{4,8},{8,12},{1,5},{5,9},{9,13},{2,6},{6,10},{10,14},{3,7},{... | collective-permute-start | bytes 196616 | tf_op jit(solution)/shard_map/ppermute | solution.py:63
  137.0 0.0 collective-permute-done.4
  137.0 0.3 fusion.6
  137.3 0.5 fusion.34
  137.8 1.1 collective-permute-done.5
  138.9 1.6 %convolution_convert_fusion.2 = bf16[8,64,128]{2,1,0:T(8,128)(2,1)} fusion(bf16[7,256,128]{2,1,0:T(8,128)(2,1)S(1)} %bitcast.64, bf16[1,256,128]{2,1,0:T(8,128)(2,1)S(1)} %bitcast.73, f32[8,64]{1,0:T(8,128)S(1)} %fusion.34, f32[8,64,256]{2,1,0:T(8,128)S(1)} %fusion.6), kind=kOutput, calls=%fused_computation.11 | convolution fusion | flops 34276096 | bytes 1181696 | tf_op jit(solution)/shard_map/cqk,ckd->cqd/dot_general | solution.py:140
  (13 shorter events, 0.2 us)
Async XLA Ops:
  6.5 87.0 %reduce-scatter.5.cloned.1.call-start = ((), (), s32[]{:S(2)}) async-start(), calls=%async_computation.6 | async-start | bytes 7864320 | tf_op jit(solution)/shard_map/reduce_scatter | solution.py:71
  34.0 3.7 %copy-start = (bf16[512,1024]{1,0:T(8,128)(2,1)S(1)}, bf16[512,1024]{1,0:T(8,128)(2,1)}, u32[]{:S(2)}) copy-start(bf16[512,1024]{1,0:T(8,128)(2,1)} %param.6) | copy-start | bytes 3145732
  34.0 23.9 %copy-start.1 = (s32[4]{0:T(128)S(1)}, s32[4]{0:T(128)}, u32[]{:S(2)}) copy-start(s32[4]{0:T(128)} %param.8) | copy-start | bytes 52
  34.0 25.1 %copy-start.2 = (s32[24]{0:T(128)S(1)}, s32[24]{0:T(128)}, u32[]{:S(2)}) copy-start(s32[24]{0:T(128)} %param.9) | copy-start | bytes 292
  34.0 63.3 %all-to-all-start = ((bf16[4,1024,128]{2,1,0:T(8,128)(2,1)}), bf16[4,1024,128]{2,1,0:T(8,128)(2,1)S(1)}, u32[]{:S(2)}, u32[]{:S(2)}) async-start(bf16[4,1024,128]{2,1,0:T(8,128)(2,1)} %bitcast), calls=%async_computation | async-start | bytes 2097152 | tf_op jit(solution)/shard_map/all_to_all | solution.py:69
  97.3 31.1 %all-to-all-start.2 = ((bf16[4,8,16384]{2,1,0:T(8,128)(2,1)}), bf16[4,8,16384]{2,1,0:T(8,128)(2,1)S(1)}, u32[]{:S(2)}, u32[]{:S(2)}) async-start(bf16[4,8,16384]{2,1,0:T(8,128)(2,1)} %fusion.1), calls=%async_computation.4 | async-start | bytes 2097152 | tf_op jit(solution)/shard_map/all_to_all | solution.py:125
  102.0 31.4 %reduce-scatter.3.cloned.1.call-start = ((), (), s32[]{:S(2)}) async-start(), calls=%async_computation.5 | async-start | bytes 1310720 | tf_op jit(solution)/shard_map/reduce_scatter | solution.py:71
  105.8 13.4 %collective-permute-start.2 = (s32[1,8]{1,0:T(1,128)S(1)}, s32[1,8]{1,0:T(1,128)S(1)}, u32[]{:S(2)}, u32[]{:S(2)}) collective-permute-start(s32[1,8]{1,0:T(1,128)S(1)} %get-tuple-element.10), channel_id=1, source_target_pairs={{0,12},{4,0},{8,4},{12,8},{1,13},{5,1},{9,5},{13,9},{2,14},{6,2},{... | collective-permute-start | bytes 104 | tf_op jit(solution)/shard_map/ppermute | solution.py:39
  109.7 18.1 %collective-permute-start.1 = (s32[1,8]{1,0:T(1,128)S(1)}, s32[1,8]{1,0:T(1,128)S(1)}, u32[]{:S(2)}, u32[]{:S(2)}) collective-permute-start(s32[1,8]{1,0:T(1,128)S(1)} %get-tuple-element.11), channel_id=1, source_target_pairs={{0,8},{4,12},{8,0},{12,4},{1,9},{5,13},{9,1},{13,5},{2,10},{6,14},... | collective-permute-start | bytes 104 | tf_op jit(solution)/shard_map/ppermute | solution.py:39
  109.7 18.1 %collective-permute-start = (s32[1,8]{1,0:T(1,128)S(1)}, s32[1,8]{1,0:T(1,128)S(1)}, u32[]{:S(2)}, u32[]{:S(2)}) collective-permute-start(s32[1,8]{1,0:T(1,128)S(1)} %get-tuple-element.12), channel_id=1, source_target_pairs={{0,4},{4,8},{8,12},{12,0},{1,5},{5,9},{9,13},{13,1},{2,6},{6,10},{... | collective-permute-start | bytes 104 | tf_op jit(solution)/shard_map/ppermute | solution.py:39
  128.8 2.0 %collective-permute-start.3 = (bf16[16,128,128]{2,1,0:T(8,128)(2,1)S(1)}, bf16[16,128,128]{2,1,0:T(8,128)(2,1)S(1)}, u32[]{:S(2)}, u32[]{:S(2)}) collective-permute-start(bf16[16,128,128]{2,1,0:T(8,128)(2,1)S(1)} %bitcast.56), channel_id=1, source_target_pairs={{0,1},{1,0},{2,3},{3,2},{4,5},{5,4},{6,7},{7,6},{8,9},{9,8},{10,11... | collective-permute-start | bytes 1572872 | tf_op jit(solution)/shard_map/ppermute | solution.py:57
  130.9 6.1 %collective-permute-start.4 = (bf16[256,128]{1,0:T(8,128)(2,1)S(1)}, bf16[256,128]{1,0:T(8,128)(2,1)S(1)}, u32[]{:S(2)}, u32[]{:S(2)}) collective-permute-start(bf16[256,128]{1,0:T(8,128)(2,1)S(1)} %bitcast.67), channel_id=1, source_target_pairs={{0,4},{4,8},{8,12},{1,5},{5,9},{9,13},{2,6},{6,10},{10,14},{3,7},{... | collective-permute-start | bytes 196616 | tf_op jit(solution)/shard_map/ppermute | solution.py:63
  134.6 4.4 %collective-permute-start.5 = (bf16[256,128]{1,0:T(8,128)(2,1)S(1)}, bf16[256,128]{1,0:T(8,128)(2,1)S(1)}, u32[]{:S(2)}, u32[]{:S(2)}) collective-permute-start(bf16[256,128]{1,0:T(8,128)(2,1)S(1)} %bitcast.68), channel_id=1, source_target_pairs={{0,4},{4,8},{8,12},{1,5},{5,9},{9,13},{2,6},{6,10},{10,14},{3,7},{... | collective-permute-start | bytes 196616 | tf_op jit(solution)/shard_map/ppermute | solution.py:63
Sparse Core Ops, SparseCore 0:
  34.1 59.3 reduce-scatter.4
  105.7 25.3 reduce-scatter.2
